TPU v7x, 32 devices: a whole 2x2x4 slice. The times are simulated.
32 devices in a mesh: tm: 16 (over z, x, core), space: 2 (over y).
Axes of the slice: x: 2, y: 2, z: 4, core: 2. Of those that a mesh axis runs over, the one named last changes fastest.
Arguments:
- conv_input: bfloat16 [16, 12, 40, 256], P('tm', None, 'space'), may hold values from -6 to 6
- conv_out: bfloat16 [16, 12, 40, 256], P('tm', None, 'space'), may hold values from -20 to 20
- kernel: bfloat16 [3, 3, 3, 256, 256], replicated, may hold values from -0.078125 to 0.078125
- gain: float32 [256], replicated, may hold values from 0.25 to 1.75
- bias: float32 [256], replicated, may hold values from -4 to 4
- cotangent: bfloat16 [16, 12, 40, 256], P('tm', None, 'space'), may hold values from -7 to 7
Outputs:
- grad_input: bfloat16 [16, 12, 40, 256], P('tm', None, 'space')
- grad_kernel: float32 [3, 3, 3, 256, 256], P(None, None, None, None, 'space')
- grad_gain: float32 [256], replicated
- grad_bias: float32 [256], replicated
All inputs are finite; a program needn't handle non-finite values.
Results may differ from a plain program's by a relative error of at most 0.0075.
Values may be sent and summed in bfloat16 or wider, within the bound.
A program may use at most 64 MiB of HBM per device.

v0:
```python
import jax
import jax.numpy as jnp
from jax import lax
from jax.sharding import PartitionSpec as P

GROUPS = 32
epsilon = 1e-06


def shifted_2(x, axis, by):
    size = lax.axis_size(axis)
    pairs = [(i, i + by) for i in range(size) if 0 <= i + by < size]
    return lax.ppermute(x, axis, pairs)


def extended_2(cells, sides, width):
    for axis, dim in sides:
        count = lax.axis_size(axis)
        ends = count - 1
        head = lax.slice_in_dim(cells, 0, width, axis=dim)
        tail = lax.slice_in_dim(cells, cells.shape[dim] - width, cells.shape[dim], axis=dim)
        cells = jnp.concatenate(
            [
                lax.ppermute(tail, axis, [(i, (i + 1) % count) for i in range(ends)]),
                cells,
                lax.ppermute(head, axis, [((i + 1) % count, i) for i in range(ends)]),
            ],
            axis=dim,
        )
    return cells


def frame_shift(block, step):
    return shifted_2(block, "tm", step)


def return_shift(block, step):
    return shifted_2(block.astype(jnp.bfloat16), "tm", step).astype(block.dtype)


def shards(conv_input, conv_out, kernel, gain, bias, cotangent):
    frames, rows, cols, chans = conv_out.shape
    width = chans // GROUPS
    grouped = conv_out.astype(jnp.float32).reshape(frames, rows, cols, GROUPS, width)
    total, square = lax.psum(
        (jnp.sum(grouped, axis=(0, 1, 2, 4)), jnp.sum(grouped * grouped, axis=(0, 1, 2, 4))),
        ("tm", "space"),
    )
    count = frames * rows * cols * width * lax.axis_size("tm") * lax.axis_size("space")
    mean = total / count
    inv_std = lax.rsqrt(square / count - mean * mean + epsilon)
    normed_grouped = (grouped - mean[:, None]) * inv_std[:, None]
    normed = normed_grouped.reshape(frames, rows, cols, chans)
    shifted = normed * gain + bias
    sigma = jax.nn.sigmoid(shifted)
    grad_shift = cotangent.astype(jnp.float32) * sigma * (1.0 + shifted * (1.0 - sigma))
    grad_grouped = (grad_shift * gain).reshape(frames, rows, cols, GROUPS, width)
    chan_bias, chan_gain = lax.psum(
        (jnp.sum(grad_shift, axis=(0, 1, 2)), jnp.sum(grad_shift * normed, axis=(0, 1, 2))),
        ("tm", "space"),
    )
    plain = jnp.sum((chan_bias * gain).reshape(GROUPS, width), axis=1)
    product = jnp.sum((chan_gain * gain).reshape(GROUPS, width), axis=1)
    grad_conv = inv_std[:, None] * (
        grad_grouped - plain[:, None] / count - normed_grouped * product[:, None] / count
    )
    grad_conv = grad_conv.reshape(frames, rows, cols, chans).astype(jnp.bfloat16)
    reach = 2
    earlier = [frame_shift(conv_input, step) for step in range(reach, 0, -1)]
    extended = jnp.concatenate(earlier + [conv_input], axis=0)
    whole_inputs = lax.all_gather(extended, "space", axis=2, tiled=True)
    channel_grads = lax.all_to_all(grad_conv, "space", split_axis=3, concat_axis=2, tiled=True)
    padded_inputs = jnp.pad(whole_inputs, ((0, 0), (1, 1), (1, 1), (0, 0)))
    wide = channel_grads.shape[2]
    contract = (((0, 1, 2), (0, 1, 2)), ((), ()))
    taps = []
    for tap_t in range(3):
        for tap_h in range(3):
            for tap_w in range(3):
                source = padded_inputs[
                    tap_t : tap_t + frames, tap_h : tap_h + rows, tap_w : tap_w + wide
                ]
                taps.append(
                    lax.dot_general(
                        source, channel_grads, contract, preferred_element_type=jnp.float32
                    )
                )
    local_kernel = jnp.stack(taps).reshape(3, 3, 3, chans, channel_grads.shape[3])
    rimmed = extended_2(grad_conv, (("space", 2),), 1)
    padded = jnp.pad(rimmed, ((0, 0), (1, 1), (0, 0), (0, 0)))
    transpose = (((3,), (1,)), ((), ()))
    partial_sums = jnp.zeros((frames + 2, rows, cols, chans), jnp.float32)
    for tap_t in range(3):
        section = jnp.zeros((frames, rows, cols, chans), jnp.float32)
        for tap_h in range(3):
            for tap_w in range(3):
                window = padded[:, 2 - tap_h : 2 - tap_h + rows, 2 - tap_w : 2 - tap_w + cols]
                section = section + lax.dot_general(
                    window,
                    kernel[tap_t, tap_h, tap_w],
                    transpose,
                    preferred_element_type=jnp.float32,
                )
        partial_sums = partial_sums.at[tap_t : tap_t + frames].add(section)
    local_part = partial_sums[2:]
    local_part = (
        local_part + return_shift(partial_sums[0:1], -2) + return_shift(partial_sums[1:2], -1)
    )
    grad_input = local_part.astype(jnp.bfloat16)
    grad_kernel = lax.psum(local_kernel, "tm")
    return (grad_input, grad_kernel, chan_gain, chan_bias)


def solution(mesh):
    return jax.shard_map(
        shards,
        mesh=mesh,
        in_specs=(
            P("tm", None, "space", None),
            P("tm", None, "space", None),
            P(),
            P(),
            P(),
            P("tm", None, "space", None),
        ),
        out_specs=(P("tm", None, "space", None), P(None, None, None, None, "space"), P(), P()),
        check_vma=False,
    )
```

profile of v0, /device:TPU:0, one launch (start us, length us, event | category | flops | bytes accessed | tf_op | source)
XLA Modules:
  0.0 271.4 jit_solution(3972550199970189502)
XLA Ops:
  7.2 0.9 copy.12
  8.1 2.4 collective-permute-start.5
  10.5 1.0 fusion.39
  11.9 4.4 %collective-permute-start.4 = (bf16[1,12,20,256]{3,1,0,2:T(8,128)(2,1)S(1)}, bf16[1,12,20,256]{3,1,0,2:T(8,128)(2,1)S(1)}, u32[]{:S(2)}, u32[]{:S(2)}) collective-permute-start(bf16[1,12,20,256]{3,1,0,2:T(8,128)(2,1)S(1)} %copy.12), channel_id=1, source_target_pairs={{0,4},{2,6},{4,8},{6,10},{8,12},{10,14},{12,16},{14,18},{16,20},{1... | collective-permute-start | bytes 368648 | tf_op jit(solution)/shard_map/ppermute | solution.py:13
  16.3 40.7 %all-reduce.3 = (f32[32]{0:T(128)S(1)}, f32[32]{0:T(128)S(1)}) all-reduce(f32[32]{0:T(128)S(1)} %reduce_sum.73, f32[32]{0:T(128)S(1)} %reduce_sum.70), channel_id=1, replica_groups=mesh['tm'=16,'space'=2] {'tm','space'}, use_global_device_ids=true, to_apply=%region_5.0 | all-reduce | flops 64 | bytes 512 | tf_op jit(solution)/shard_map/psum | solution.py:45
  57.4 1.2 fusion.214
  58.6 39.8 %all-reduce.2 = (f32[256]{0:T(256)S(1)}, f32[256]{0:T(256)S(1)}) all-reduce(f32[256]{0:T(256)S(1)} %get-tuple-element.41, f32[256]{0:T(256)S(1)} %get-tuple-element.40), channel_id=1, replica_groups=mesh['tm'=16,'space'=2] {'tm','space'}, use_global_device_ids=true, to_apply=%region_10.11 | all-reduce | flops 512 | bytes 4096 | tf_op jit(solution)/shard_map/psum | solution.py:58
  98.4 0.7 fusion.217
  99.8 1.0 fusion.56
  100.9 4.2 %collective-permute-start = (bf16[1,12,1,256]{3,2,1,0:T(2,128)(2,1)S(1)}, bf16[1,12,1,256]{3,2,1,0:T(2,128)(2,1)S(1)}, u32[]{:S(2)}, u32[]{:S(2)}) collective-permute-start(bf16[1,12,1,256]{3,2,1,0:T(2,128)(2,1)S(1)} %get-tuple-element.49), channel_id=1, source_target_pairs={{0,1},{2,3},{4,5},{6,7},{8,9},{10,11},{12,13},{14,15},{16,17},{18,... | collective-permute-start | bytes 18440 | tf_op jit(solution)/shard_map/ppermute | solution.py:24
  105.1 1.3 collective-permute-start.1
  106.4 1.0 copy.16
  107.4 1.8 reshape.522
  109.1 3.9 %all-to-all-start = ((bf16[2,2,15360]{2,1,0:T(2,128)(2,1)}), bf16[2,2,15360]{2,1,0:T(2,128)(2,1)S(1)}, u32[]{:S(2)}, u32[]{:S(2)}) async-start(bf16[2,2,15360]{2,1,0:T(2,128)(2,1)} %reshape.522), calls=%async_computation | async-start | bytes 245760 | tf_op jit(solution)/shard_map/all_to_all | solution.py:72
  113.1 1.3 fusion.114
  114.3 1.1 fusion.112
  115.5 1.1 fusion.116
  116.7 1.1 fusion.131
  117.9 1.1 fusion.120
  119.0 1.1 fusion.138
  122.5 1.3 collective-permute-start.2
  124.8 1.3 collective-permute-start.3
  126.1 1.1 reshape.523
  127.3 0.8 copy.17
  128.2 14.7 %all_gather.3 = bf16[3,12,40,256]{3,1,0,2:T(8,128)(2,1)S(1)} all-gather(bf16[3,12,20,256]{3,1,0,2:T(8,128)(2,1)S(1)} %pad_maximum_fusion), channel_id=1, replica_groups=mesh['tm'=16,'space'=2] {'space'}, dimensions={2}, use_global_device_ids=true | all-gather | bytes 1105920 | tf_op jit(solution)/shard_map/all_gather | solution.py:71
  143.6 0.3 fusion.35
  144.4 0.3 fusion.32
  144.6 0.3 fusion.31
  145.2 0.3 fusion.29
  145.4 0.3 fusion.28
  146.0 0.3 fusion.26
  146.8 0.3 fusion.23
  147.0 0.3 fusion.22
  147.6 0.3 fusion.20
  148.4 0.3 fusion.17
  149.2 0.3 fusion.14
  149.4 0.3 fusion.13
  150.2 1.8 copy-done
  152.0 1.1 fusion.149
  153.2 1.1 convolution_add_fusion.17
  154.3 1.1 convolution_add_fusion.16
  155.5 1.1 fusion.6
  156.6 1.1 fusion.5
  157.8 1.1 convolution_add_fusion.13
  158.9 1.2 fusion.4
  160.1 0.7 add_convert_fusion
  160.8 99.6 %all-reduce.6.cloned.1.call-done = f32[3,3,3,256,128]{4,3,2,1,0:T(8,128)} async-done(((f32[3,3,3,256,128]{4,3,2,1,0:T(8,128)}), f32[3,3,3,256,128]{4,3,2,1,0:T(8,128)}) %all-reduce.6.cloned.1.call-update) | async-done | bytes 3538960 | tf_op jit(solution)/shard_map/psum | solution.py:110
  260.4 4.2 %copy.48 = f32[3,3,3,256,128]{4,3,2,1,0:T(8,128)} copy(f32[3,3,3,256,128]{4,3,2,1,0:T(8,128)} %all-reduce.6.cloned.1.call-done) | data formatting | bytes 7077888
  (68 shorter events, 9.1 us)
Async XLA Ops:
  8.1 120.0 %collective-permute-start.5 = (bf16[1,12,20,256]{3,1,0,2:T(8,128)(2,1)S(1)}, bf16[1,12,20,256]{3,1,0,2:T(8,128)(2,1)S(1)}, u32[]{:S(2)}, u32[]{:S(2)}) collective-permute-start(bf16[1,12,20,256]{3,1,0,2:T(8,128)(2,1)S(1)} %copy.12), channel_id=1, source_target_pairs={{0,2},{2,4},{4,6},{6,8},{8,10},{10,12},{12,14},{14,16},{16,18},{18... | collective-permute-start | bytes 368648 | tf_op jit(solution)/shard_map/ppermute | solution.py:13
  11.9 116.2 %collective-permute-start.4 = (bf16[1,12,20,256]{3,1,0,2:T(8,128)(2,1)S(1)}, bf16[1,12,20,256]{3,1,0,2:T(8,128)(2,1)S(1)}, u32[]{:S(2)}, u32[]{:S(2)}) collective-permute-start(bf16[1,12,20,256]{3,1,0,2:T(8,128)(2,1)S(1)} %copy.12), channel_id=1, source_target_pairs={{0,4},{2,6},{4,8},{6,10},{8,12},{10,14},{12,16},{14,18},{16,20},{1... | collective-permute-start | bytes 368648 | tf_op jit(solution)/shard_map/ppermute | solution.py:13
  98.4 21.8 %copy-start.2 = (f32[256]{0:T(256)}, f32[256]{0:T(256)S(1)}, u32[]{:S(2)}) copy-start(f32[256]{0:T(256)S(1)} %get-tuple-element.57) | copy-start | bytes 3076
  98.4 21.8 %copy-start.3 = (f32[256]{0:T(256)}, f32[256]{0:T(256)S(1)}, u32[]{:S(2)}) copy-start(f32[256]{0:T(256)S(1)} %get-tuple-element.58) | copy-start | bytes 3076
  100.9 15.7 %collective-permute-start = (bf16[1,12,1,256]{3,2,1,0:T(2,128)(2,1)S(1)}, bf16[1,12,1,256]{3,2,1,0:T(2,128)(2,1)S(1)}, u32[]{:S(2)}, u32[]{:S(2)}) collective-permute-start(bf16[1,12,1,256]{3,2,1,0:T(2,128)(2,1)S(1)} %get-tuple-element.49), channel_id=1, source_target_pairs={{0,1},{2,3},{4,5},{6,7},{8,9},{10,11},{12,13},{14,15},{16,17},{18,... | collective-permute-start | bytes 18440 | tf_op jit(solution)/shard_map/ppermute | solution.py:24
  105.1 11.6 %collective-permute-start.1 = (bf16[1,12,1,256]{3,2,1,0:T(2,128)(2,1)S(1)}, bf16[1,12,1,256]{3,2,1,0:T(2,128)(2,1)S(1)}, u32[]{:S(2)}, u32[]{:S(2)}) collective-permute-start(bf16[1,12,1,256]{3,2,1,0:T(2,128)(2,1)S(1)} %get-tuple-element.50), channel_id=1, source_target_pairs={{1,0},{3,2},{5,4},{7,6},{9,8},{11,10},{13,12},{15,14},{17,16},{19,... | collective-permute-start | bytes 18440 | tf_op jit(solution)/shard_map/ppermute | solution.py:26
  109.1 16.9 %all-to-all-start = ((bf16[2,2,15360]{2,1,0:T(2,128)(2,1)}), bf16[2,2,15360]{2,1,0:T(2,128)(2,1)S(1)}, u32[]{:S(2)}, u32[]{:S(2)}) async-start(bf16[2,2,15360]{2,1,0:T(2,128)(2,1)} %reshape.522), calls=%async_computation | async-start | bytes 245760 | tf_op jit(solution)/shard_map/all_to_all | solution.py:72
  113.1 147.4 %all-reduce.6.cloned.1.call-start = ((), (), s32[]{:S(2)}) async-start(), calls=%async_computation.1 | async-start | bytes 7077888 | tf_op jit(solution)/shard_map/psum | solution.py:110
  113.1 7.1 %copy-start.1 = (bf16[3,3,3,256,256]{4,3,2,1,0:T(8,128)(2,1)S(1)}, bf16[3,3,3,256,256]{4,3,2,1,0:T(8,128)(2,1)}, u32[]{:S(2)}) copy-start(bf16[3,3,3,256,256]{4,3,2,1,0:T(8,128)(2,1)} %param.14) | copy-start | bytes 10616836
  122.5 37.6 %collective-permute-start.2 = (bf16[1,12,20,256]{3,2,1,0:T(8,128)(2,1)S(1)}, bf16[1,12,20,256]{3,2,1,0:T(8,128)(2,1)S(1)}, u32[]{:S(2)}, u32[]{:S(2)}) collective-permute-start(bf16[1,12,20,256]{3,2,1,0:T(8,128)(2,1)S(1)} %fusion.10), channel_id=1, source_target_pairs={{4,0},{6,2},{8,4},{10,6},{12,8},{14,10},{16,12},{18,14},{20,16},{2... | collective-permute-start | bytes 368648 | tf_op jit(solution)/shard_map/ppermute | solution.py:13
  124.8 35.3 %collective-permute-start.3 = (bf16[1,12,20,256]{3,2,1,0:T(8,128)(2,1)S(1)}, bf16[1,12,20,256]{3,2,1,0:T(8,128)(2,1)S(1)}, u32[]{:S(2)}, u32[]{:S(2)}) collective-permute-start(bf16[1,12,20,256]{3,2,1,0:T(8,128)(2,1)S(1)} %fusion.9), channel_id=1, source_target_pairs={{2,0},{4,2},{6,4},{8,6},{10,8},{12,10},{14,12},{16,14},{18,16},{20... | collective-permute-start | bytes 368648 | tf_op jit(solution)/shard_map/ppermute | solution.py:13
  150.2 1.8 copy-start
Sparse Core Ops, SparseCore 0:
  152.2 108.2 all-reduce.5
where the time goes:
time: 272 us; the launch traced here: 271 us
  waiting for transfers between devices  99.6 us (37%)
  blocking collectives  95.2 us (35%)
  matrix products  25.2 us (9%)
  starting transfers between devices  18.8 us (7%)
  between operations  14.5 us (5%)
  local copies, waits for them, and re-layouts  12.9 us (5%)
  other arithmetic  5.27 us (2%)
    psum x1, waiting for transfers between devices, shards(): grad_kernel = lax.psum(local_kernel, 'tm')  99.6 us
    psum x1, blocking collectives, shards(): lax.psum((jnp.sum(grouped, axis=(0, 1, 2, 4)), jnp.sum(grouped * grouped,...  40.7 us
    psum x1, blocking collectives, shards(): lax.psum((jnp.sum(grad_shift, axis=(0, 1, 2)), jnp.sum(grad_shift * norme...  39.8 us
    dot_general x27, matrix products, shards(): lax.dot_general(window, kernel[tap_t, tap_h, tap_w], transpose, preferred...  18.1 us
    all_gather x1, blocking collectives, shards(): whole_inputs = lax.all_gather(extended, 'space', axis=2, tiled=True)  14.7 us
    unnamed x12, local copies, waits for them, and re-layouts  9.84 us
    ppermute x4, starting transfers between devices, shifted_2(): return lax.ppermute(x, axis, pairs)  9.39 us
    dot_general x27, matrix products, shards(): lax.dot_general(source, channel_grads, contract, preferred_element_type=j...  7.09 us
  transfers between devices with their start and end apart: 8, of which 1 were waited for; matrix products, arithmetic and copies ran while one was open for 13% of the time, Pallas kernels for 0%

commit v1 on v0

--- a/solution.py
+++ b/solution.py
@@ -1,3 +1,4 @@
+import functools
 import jax
 import jax.numpy as jnp
 from jax import lax
@@ -5,6 +6,20 @@
 
 GROUPS = 32
 epsilon = 1e-06
+
+
+def lead_ports(vec, dev_axis):
+    n = jax.lax.psum(1, dev_axis)
+    z_new = lambda passed: [(tick, tick ^ passed) for tick in range(n)]
+    state_next = vec
+    for w in range(n.bit_length() - 1):
+        state_next = state_next + jax.lax.ppermute(
+            state_next, axis_name=dev_axis, perm=z_new(1 << w)
+        )
+    return state_next
+
+
+note_the_group = functools.partial(lead_ports, dev_axis="tm")
 
 
 def shifted_2(x, axis, by):
@@ -107,7 +122,7 @@
         local_part + return_shift(partial_sums[0:1], -2) + return_shift(partial_sums[1:2], -1)
     )
     grad_input = local_part.astype(jnp.bfloat16)
-    grad_kernel = lax.psum(local_kernel, "tm")
+    grad_kernel = note_the_group(local_kernel)
     return (grad_input, grad_kernel, chan_gain, chan_bias)
 
 

time: 272 us -> 448 us (1.65)
  waiting for transfers between devices: 99.6 us -> 299 us
  between operations: 14.5 us -> 1.12 us
  matrix products: 25.2 us -> 13.3 us
  local copies, waits for them, and re-layouts: 12.9 us -> 6.25 us
    ppermute x0 -> x4, waiting for transfers between devices: none -> 294 us  [lead_ports(): jax.lax.ppermute(state_next, axis_name=dev_axis, perm=z_new(1 << w))]
    psum x1 -> x0, waiting for transfers between devices: 99.6 us -> none  [shards(): grad_kernel = lax.psum(local_kernel, 'tm')]
    dot_general x27, matrix products: 18.1 us -> 6.2 us  [shards(): lax.dot_general(window, kernel[tap_t, tap_h, tap_w], transpose, preferred...]
    all_to_all x0 -> x1, blocking collectives: none -> 7.76 us  [shards(): lax.all_to_all(grad_conv, 'space', split_axis=3, concat_axis=2, tiled=True)]
    unnamed x12 -> x9, local copies, waits for them, and re-layouts: 9.84 us -> 3.22 us
    ppermute x0 -> x4, starting transfers between devices: none -> 5.23 us  [lead_ports(): jax.lax.ppermute(state_next, axis_name=dev_axis, perm=z_new(1 << w))]
  transfers between devices with their start and end apart: 8 -> 10, of which waited for: 1 -> 6; matrix products, arithmetic and copies ran while one was open for 13% -> 4% of each run, Pallas kernels for 0% -> 0%
where the time goes in v1:
time: 448 us; the launch traced here: 446 us
  waiting for transfers between devices  299 us (67%)
  blocking collectives  99.1 us (22%)
  starting transfers between devices  18.1 us (4%)
  matrix products  13.3 us (3%)
  other arithmetic  8.95 us (2%)
  local copies, waits for them, and re-layouts  6.25 us (1%)
    ppermute x4, waiting for transfers between devices, lead_ports(): jax.lax.ppermute(state_next, axis_name=dev_axis, perm=z_new(1 << w))  294 us
    psum x1, blocking collectives, shards(): lax.psum((jnp.sum(grouped, axis=(0, 1, 2, 4)), jnp.sum(grouped * grouped,...  40.7 us
    psum x1, blocking collectives, shards(): lax.psum((jnp.sum(grad_shift, axis=(0, 1, 2)), jnp.sum(grad_shift * norme...  39.8 us
    all_gather x1, blocking collectives, shards(): whole_inputs = lax.all_gather(extended, 'space', axis=2, tiled=True)  10.9 us
    ppermute x4, starting transfers between devices, shifted_2(): return lax.ppermute(x, axis, pairs)  9.39 us
  transfers between devices with their start and end apart: 10, of which 6 were waited for; matrix products, arithmetic and copies ran while one was open for 4% of the time, Pallas kernels for 0%

profile of v1, /device:TPU:0, one launch (start us, length us, event | category | flops | bytes accessed | tf_op | source)
XLA Modules:
  0.0 445.6 jit_solution(593519723730391502)
XLA Ops:
  0.6 0.9 copy.12
  1.6 2.4 collective-permute-start.5
  4.0 1.0 fusion.39
  5.4 4.4 collective-permute-start.4
  9.8 40.7 %all-reduce.3 = (f32[32]{0:T(128)S(1)}, f32[32]{0:T(128)S(1)}) all-reduce(f32[32]{0:T(128)S(1)} %reduce_sum.73, f32[32]{0:T(128)S(1)} %reduce_sum.70), channel_id=1, replica_groups=mesh['tm'=16,'space'=2] {'tm','space'}, use_global_device_ids=true, to_apply=%region_5.0 | all-reduce | flops 64 | bytes 512 | tf_op jit(solution)/shard_map/psum | solution.py:60
  50.8 1.2 fusion.214
  52.0 39.8 %all-reduce.2 = (f32[256]{0:T(256)S(1)}, f32[256]{0:T(256)S(1)}) all-reduce(f32[256]{0:T(256)S(1)} %get-tuple-element.41, f32[256]{0:T(256)S(1)} %get-tuple-element.40), channel_id=1, replica_groups=mesh['tm'=16,'space'=2] {'tm','space'}, use_global_device_ids=true, to_apply=%region_10.11 | all-reduce | flops 512 | bytes 4096 | tf_op jit(solution)/shard_map/psum | solution.py:73
  91.8 0.7 fusion.217
  93.3 1.0 fusion.56
  94.3 1.0 copy.16
  95.3 1.1 reshape.522
  96.4 7.8 %all_to_all.15 = bf16[2,2,15360]{2,1,0:T(2,128)(2,1)S(1)} all-to-all(bf16[2,2,15360]{2,1,0:T(2,128)(2,1)S(1)} %reshape.522), channel_id=1, replica_groups=mesh['tm'=16,'space'=2] {'space'}, dimensions={0} | all-to-all | bytes 245760 | tf_op jit(solution)/shard_map/all_to_all | solution.py:87
  104.2 1.1 reshape.523
  105.3 0.8 copy.17
  106.2 10.9 %all_gather.3 = bf16[3,12,40,256]{3,1,0,2:T(8,128)(2,1)S(1)} all-gather(bf16[3,12,20,256]{3,1,0,2:T(8,128)(2,1)S(1)} %pad_maximum_fusion), channel_id=1, replica_groups=mesh['tm'=16,'space'=2] {'space'}, dimensions={2}, use_global_device_ids=true | all-gather | bytes 1105920 | tf_op jit(solution)/shard_map/all_gather | solution.py:86
  117.9 0.3 fusion.35
  118.2 0.3 fusion.34
  118.7 0.3 fusion.32
  119.0 0.3 fusion.31
  119.5 0.3 fusion.29
  119.8 0.3 fusion.28
  120.3 0.3 fusion.26
  121.1 0.3 fusion.23
  121.4 0.3 fusion.22
  121.9 0.3 fusion.20
  122.2 0.3 fusion.19
  122.7 0.3 fusion.17
  123.5 0.3 fusion.14
  123.8 0.3 fusion.13
  124.3 0.3 fusion.11
  124.6 6.2 %collective-permute-done.6 = f32[3,3,3,256,128]{4,3,2,1,0:T(8,128)S(1)} collective-permute-done((f32[3,3,3,256,128]{4,3,2,1,0:T(8,128)S(1)}, f32[3,3,3,256,128]{4,3,2,1,0:T(8,128)S(1)}, u32[]{:S(2)}, u32[]{:S(2)}) %collective-permute-start.6) | collective-permute-done | bytes 3538976 | tf_op jit(solution)/shard_map/ppermute | solution.py:16
  130.8 0.5 add.204
  131.4 1.5 collective-permute-start.7
  132.8 77.1 %collective-permute-done.7 = f32[3,3,3,256,128]{4,3,2,1,0:T(8,128)S(1)} collective-permute-done((f32[3,3,3,256,128]{4,3,2,1,0:T(8,128)S(1)}, f32[3,3,3,256,128]{4,3,2,1,0:T(8,128)S(1)}, u32[]{:S(2)}, u32[]{:S(2)}) %collective-permute-start.7) | collective-permute-done | bytes 3538976 | tf_op jit(solution)/shard_map/ppermute | solution.py:16
  210.0 0.5 add.205
  210.5 1.5 collective-permute-start.8
  212.0 2.2 collective-permute-start
  214.2 1.3 collective-permute-start.1
  216.2 3.6 collective-permute-done.1
  222.0 66.2 %collective-permute-done.8 = f32[3,3,3,256,128]{4,3,2,1,0:T(8,128)S(1)} collective-permute-done((f32[3,3,3,256,128]{4,3,2,1,0:T(8,128)S(1)}, f32[3,3,3,256,128]{4,3,2,1,0:T(8,128)S(1)}, u32[]{:S(2)}, u32[]{:S(2)}) %collective-permute-start.8) | collective-permute-done | bytes 3538976 | tf_op jit(solution)/shard_map/ppermute | solution.py:16
  288.2 0.5 add.206
  288.7 2.2 collective-permute-start.9
  291.1 1.3 collective-permute-start.2
  293.9 1.3 collective-permute-start.3
  297.1 1.1 collective-permute-done.2
  298.2 0.7 add_convert_fusion
  298.9 144.5 %collective-permute-done.9 = f32[3,3,3,256,128]{4,3,2,1,0:T(8,128)S(1)} collective-permute-done((f32[3,3,3,256,128]{4,3,2,1,0:T(8,128)S(1)}, f32[3,3,3,256,128]{4,3,2,1,0:T(8,128)S(1)}, u32[]{:S(2)}, u32[]{:S(2)}) %collective-permute-start.9) | collective-permute-done | bytes 3538976 | tf_op jit(solution)/shard_map/ppermute | solution.py:16
  443.4 2.2 add.207
  (73 shorter events, 11.3 us)
Async XLA Ops:
  1.6 104.6 %collective-permute-start.5 = (bf16[1,12,20,256]{3,1,0,2:T(8,128)(2,1)S(1)}, bf16[1,12,20,256]{3,1,0,2:T(8,128)(2,1)S(1)}, u32[]{:S(2)}, u32[]{:S(2)}) collective-permute-start(bf16[1,12,20,256]{3,1,0,2:T(8,128)(2,1)S(1)} %copy.12), channel_id=1, source_target_pairs={{0,2},{2,4},{4,6},{6,8},{8,10},{10,12},{12,14},{14,16},{16,18},{18... | collective-permute-start | bytes 368648 | tf_op jit(solution)/shard_map/ppermute | solution.py:28
  5.4 100.8 %collective-permute-start.4 = (bf16[1,12,20,256]{3,1,0,2:T(8,128)(2,1)S(1)}, bf16[1,12,20,256]{3,1,0,2:T(8,128)(2,1)S(1)}, u32[]{:S(2)}, u32[]{:S(2)}) collective-permute-start(bf16[1,12,20,256]{3,1,0,2:T(8,128)(2,1)S(1)} %copy.12), channel_id=1, source_target_pairs={{0,4},{2,6},{4,8},{6,10},{8,12},{10,14},{12,16},{14,18},{16,20},{1... | collective-permute-start | bytes 368648 | tf_op jit(solution)/shard_map/ppermute | solution.py:28
  91.8 25.3 %copy-start.1 = (f32[256]{0:T(256)}, f32[256]{0:T(256)S(1)}, u32[]{:S(2)}) copy-start(f32[256]{0:T(256)S(1)} %get-tuple-element.44) | copy-start | bytes 3076
  91.8 25.3 %copy-start.2 = (f32[256]{0:T(256)}, f32[256]{0:T(256)S(1)}, u32[]{:S(2)}) copy-start(f32[256]{0:T(256)S(1)} %get-tuple-element.45) | copy-start | bytes 3076
  124.5 6.3 %collective-permute-start.6 = (f32[3,3,3,256,128]{4,3,2,1,0:T(8,128)S(1)}, f32[3,3,3,256,128]{4,3,2,1,0:T(8,128)S(1)}, u32[]{:S(2)}, u32[]{:S(2)}) collective-permute-start(f32[3,3,3,256,128]{4,3,2,1,0:T(8,128)S(1)} %bitcast.438), channel_id=1, source_target_pairs={{0,2},{2,0},{4,6},{6,4},{8,10},{10,8},{12,14},{14,12},{16,18},{18,... | collective-permute-start | bytes 10616840 | tf_op jit(solution)/shard_map/ppermute | solution.py:16
  131.3 84.2 %copy-start = (bf16[3,3,3,256,256]{4,3,2,1,0:T(8,128)(2,1)S(1)}, bf16[3,3,3,256,256]{4,3,2,1,0:T(8,128)(2,1)}, u32[]{:S(2)}) copy-start(bf16[3,3,3,256,256]{4,3,2,1,0:T(8,128)(2,1)} %param.14) | copy-start | bytes 10616836
  131.4 78.6 %collective-permute-start.7 = (f32[3,3,3,256,128]{4,3,2,1,0:T(8,128)S(1)}, f32[3,3,3,256,128]{4,3,2,1,0:T(8,128)S(1)}, u32[]{:S(2)}, u32[]{:S(2)}) collective-permute-start(f32[3,3,3,256,128]{4,3,2,1,0:T(8,128)S(1)} %add.204), channel_id=1, source_target_pairs={{0,4},{2,6},{4,0},{6,2},{8,12},{10,14},{12,8},{14,10},{16,20},{18,... | collective-permute-start | bytes 10616840 | tf_op jit(solution)/shard_map/ppermute | solution.py:16
  210.5 77.8 %collective-permute-start.8 = (f32[3,3,3,256,128]{4,3,2,1,0:T(8,128)S(1)}, f32[3,3,3,256,128]{4,3,2,1,0:T(8,128)S(1)}, u32[]{:S(2)}, u32[]{:S(2)}) collective-permute-start(f32[3,3,3,256,128]{4,3,2,1,0:T(8,128)S(1)} %add.205), channel_id=1, source_target_pairs={{0,8},{2,10},{4,12},{6,14},{8,0},{10,2},{12,4},{14,6},{16,24},{18,... | collective-permute-start | bytes 10616840 | tf_op jit(solution)/shard_map/ppermute | solution.py:16
  212.0 4.2 collective-permute-start
  214.2 5.6 %collective-permute-start.1 = (bf16[1,12,1,256]{3,2,1,0:T(2,128)(2,1)S(1)}, bf16[1,12,1,256]{3,2,1,0:T(2,128)(2,1)S(1)}, u32[]{:S(2)}, u32[]{:S(2)}) collective-permute-start(bf16[1,12,1,256]{3,2,1,0:T(2,128)(2,1)S(1)} %get-tuple-element.50), channel_id=1, source_target_pairs={{1,0},{3,2},{5,4},{7,6},{9,8},{11,10},{13,12},{15,14},{17,16},{19,... | collective-permute-start | bytes 18440 | tf_op jit(solution)/shard_map/ppermute | solution.py:41
  288.7 154.6 %collective-permute-start.9 = (f32[3,3,3,256,128]{4,3,2,1,0:T(8,128)S(1)}, f32[3,3,3,256,128]{4,3,2,1,0:T(8,128)S(1)}, u32[]{:S(2)}, u32[]{:S(2)}) collective-permute-start(f32[3,3,3,256,128]{4,3,2,1,0:T(8,128)S(1)} %add.206), channel_id=1, source_target_pairs={{0,16},{2,18},{4,20},{6,22},{8,24},{10,26},{12,28},{14,30},{16,0},... | collective-permute-start | bytes 10616840 | tf_op jit(solution)/shard_map/ppermute | solution.py:16
  291.1 7.0 %collective-permute-start.2 = (bf16[1,12,20,256]{3,2,1,0:T(8,128)(2,1)S(1)}, bf16[1,12,20,256]{3,2,1,0:T(8,128)(2,1)S(1)}, u32[]{:S(2)}, u32[]{:S(2)}) collective-permute-start(bf16[1,12,20,256]{3,2,1,0:T(8,128)(2,1)S(1)} %fusion.10), channel_id=1, source_target_pairs={{4,0},{6,2},{8,4},{10,6},{12,8},{14,10},{16,12},{18,14},{20,16},{2... | collective-permute-start | bytes 368648 | tf_op jit(solution)/shard_map/ppermute | solution.py:28
  293.9 4.3 collective-permute-start.3
